TPU v7x, 128 devices: a whole 4x4x4 slice. The times are simulated.
128 devices in a mesh: space: 8 (over x, core), win: 16 (over z, y).
Axes of the slice: x: 4, y: 4, z: 4, core: 2. Of those that a mesh axis runs over, the one named last changes fastest.
Arguments:
- snapshots: bfloat16 [128, 24576, 256], P('win', 'space'), as said below
- modes: bfloat16 [128, 24576, 256], P('win', 'space'), may hold values from -0.5 to 0.5
- amp_re: float32 [128, 128], P('win'), may hold values from -5 to 5
- amp_im: float32 [128, 128], P('win'), may hold values from -5 to 5
- growth: float32 [128, 128], P('win'), may hold values from -0.01171875 to 0.001953125
- freq: float32 [128, 128], P('win'), may hold values from -3.140625 to 3.140625
- mode_count: int32 [128], P('win'), may hold values from 8 to 128
- slot_window: int32 [128], P('win'), may hold values from 0 to 127, as said below
Outputs:
- gram: float32 [128, 256, 256], P('win')
Inputs may be any that keep to these rules, and one draw needn't show every extreme that they name: slot_window is a permutation of the 128 windows; slot j holds a window of the same position in its block, slot_window[j] % 8 == j % 8; the 8 slots of one block hold windows of 8 different blocks. Each point's snapshots share one scale.
All inputs are finite; a program needn't handle non-finite values.
Results may differ from a plain program's by a relative error of at most 0.0026.
Values may be sent and summed in bfloat16 or wider, within the bound.
A program may use at most 192 MiB of HBM per device.

v0:
```python
import jax
import jax.numpy as jnp
from jax import lax
from jax.sharding import PartitionSpec as P

K = 128
S = 256
WIN_DEV = 8


def coefficients(amp_re, amp_im, growth, freq, mode_count):
    steps = jnp.arange(S).astype(jnp.float32)
    live = (jnp.arange(K, dtype=jnp.int32)[None, :] < mode_count[:, None]).astype(jnp.float32)
    decay = jnp.exp(growth[:, :, None] * steps) * live[:, :, None]
    angle = freq[:, :, None] * steps
    cosine = jnp.cos(angle)
    sine = jnp.sin(angle)
    real_part = (amp_re[:, :, None] * cosine - amp_im[:, :, None] * sine) * decay
    imag_part = (amp_re[:, :, None] * sine + amp_im[:, :, None] * cosine) * decay
    stacked = jnp.stack([real_part, -imag_part], axis=2)
    return stacked.reshape(amp_re.shape[0], 2 * K, S).astype(jnp.bfloat16)


def batch_grams(slabs, vectors, coef):
    recon = jnp.einsum("wpk,wks->wps", vectors, coef, preferred_element_type=jnp.float32)
    resid = (slabs.astype(jnp.float32) - recon).astype(jnp.bfloat16)
    return jnp.einsum("wps,wpt->wst", resid, resid, preferred_element_type=jnp.float32)


def on_device(snapshots, modes, amp_re, amp_im, growth, freq, mode_count, slot_window):
    nblocks = lax.axis_size("win")
    points_all = snapshots.shape[1] * lax.axis_size("space")
    coef = coefficients(amp_re, amp_im, growth, freq, mode_count)
    dest = slot_window // WIN_DEV
    place = slot_window % WIN_DEV
    vec_buf = jnp.zeros((nblocks,) + modes.shape[1:], jnp.bfloat16).at[dest].set(modes)
    coef_buf = jnp.zeros((nblocks, 2 * K, S), jnp.bfloat16).at[dest].set(coef)
    mark_buf = (
        jnp.zeros((nblocks, 128), jnp.bfloat16)
        .at[dest, place]
        .set(jnp.ones((WIN_DEV,), jnp.bfloat16))
    )
    got_vec, got_coef, got_mark = (
        lax.all_to_all(vec_buf, "win", split_axis=0, concat_axis=0, tiled=True),
        lax.all_to_all(coef_buf, "win", split_axis=0, concat_axis=0, tiled=True),
        lax.all_to_all(mark_buf, "win", split_axis=0, concat_axis=0, tiled=True),
    )
    marks = got_mark[:, :WIN_DEV].astype(jnp.int32)
    source = jnp.sum(jnp.arange(nblocks, dtype=jnp.int32)[:, None] * marks, axis=0)
    partial_value = batch_grams(snapshots, got_vec[source], got_coef[source])
    total = lax.psum(partial_value, "space")
    return total / points_all


def solution(mesh):
    return jax.shard_map(
        on_device,
        mesh=mesh,
        in_specs=(
            P("win", "space", None),
            P("win", "space", None),
            P("win", None),
            P("win", None),
            P("win", None),
            P("win", None),
            P("win"),
            P("win"),
        ),
        out_specs=P("win", None, None),
        check_vma=False,
    )
```

profile of v0, /device:TPU:0, one launch (start us, length us, event | category | flops | bytes accessed | tf_op | source)
XLA Modules:
  0.0 555.7 jit_solution(11417734754348130964)
XLA Ops:
  6.5 0.7 fusion.18
  7.2 0.9 scatter_fusion.1
  8.1 0.6 copy.20
  8.7 8.2 %all-to-all-start.1 = ((bf16[16,1,128]{2,1,0:T(2,128)(2,1)}), bf16[16,1,128]{2,1,0:T(2,128)(2,1)S(1)}, u32[]{:S(2)}, u32[]{:S(2)}) async-start(bf16[16,1,128]{2,1,0:T(2,128)(2,1)} %copy.20), calls=%async_computation.1 | async-start | bytes 16384 | tf_op jit(solution)/shard_map/all_to_all | solution.py:46
  16.9 0.7 fusion.14
  17.6 5.3 fusion.9
  22.9 0.1 pad_maximum_fusion
  23.1 0.6 copy.21
  23.6 0.2 copy.22
  23.9 1.5 broadcast_in_dim.14
  25.4 2.8 scatter_fusion.2
  28.2 0.0 all-to-all-done.1
  28.2 7.2 %all-to-all-start.2 = ((bf16[16,256,256]{2,1,0:T(8,128)(2,1)}), bf16[16,256,256]{2,1,0:T(8,128)(2,1)S(1)}, u32[]{:S(2)}, u32[]{:S(2)}) async-start(bf16[16,256,256]{2,1,0:T(8,128)(2,1)} %scatter_fusion.2), calls=%async_computation.2 | async-start | bytes 4194304 | tf_op jit(solution)/shard_map/all_to_all | solution.py:45
  35.5 8.3 %broadcast_in_dim.10 = bf16[16,3072,256]{2,1,0:T(8,128)(2,1)} broadcast(bf16[]{:T(256)} %constant.32.clone.1), dimensions={} | broadcast | bytes 25165826 | tf_op jit(solution)/shard_map/broadcast_in_dim | solution.py:36
  43.8 25.7 %scatter_fusion = bf16[16,3072,256]{2,1,0:T(8,128)(2,1)} fusion(bf16[16,3072,256]{2,1,0:T(8,128)(2,1)} %broadcast_in_dim.10, s32[8]{0:T(128)S(1)} %get-tuple-element.6, bf16[8,3072,256]{2,1,0:T(8,128)(2,1)} %param.9), kind=kCustom, calls=%fused_computation.2 | custom fusion | bytes 37748768 | tf_op jit(solution)/shard_map/scatter | solution.py:36
  69.5 0.0 all-to-all-done.2
  69.5 7.4 %all-to-all-start = ((bf16[16,3072,256]{2,1,0:T(8,128)(2,1)}), bf16[16,3072,256]{2,1,0:T(8,128)(2,1)}, u32[]{:S(2)}, u32[]{:S(2)}) async-start(bf16[16,3072,256]{2,1,0:T(8,128)(2,1)} %scatter_fusion), calls=%async_computation | async-start | bytes 50331648 | tf_op jit(solution)/shard_map/all_to_all | solution.py:44
  76.9 0.0 all-reduce.2.cloned.1.call-start
  77.0 0.6 gather_fusion.1
  77.6 369.2 %all-to-all-done = bf16[16,3072,256]{2,1,0:T(8,128)(2,1)} async-done(((bf16[16,3072,256]{2,1,0:T(8,128)(2,1)}), bf16[16,3072,256]{2,1,0:T(8,128)(2,1)}, u32[]{:S(2)}, u32[]{:S(2)}) %all-to-all-start) | async-done | bytes 25165856 | tf_op jit(solution)/shard_map/all_to_all | solution.py:44
  446.8 14.6 %gather_fusion = bf16[8,3072,256]{2,1,0:T(8,128)(2,1)} fusion(bf16[16,3072,256]{2,1,0:T(8,128)(2,1)} %all-to-all-done, s32[1024]{0:T(1024)S(1)} %pad_clamp_fusion), kind=kCustom, calls=%fused_computation | custom fusion | bytes 25165856 | tf_op jit(solution)/shard_map/gather | solution.py:50
  461.4 19.9 %fusion = f32[8,256,256]{2,1,0:T(8,128)} fusion(bf16[8,3072,256]{2,1,0:T(8,128)(2,1)} %param.8, bf16[8,3072,256]{2,1,0:T(8,128)(2,1)} %gather_fusion, bf16[8,256,256]{2,1,0:T(8,128)(2,1)S(1)} %gather_fusion.1), kind=kOutput, calls=%fused_computation.6 | convolution fusion | flops 6461325312 | bytes 28311552 | tf_op jit(solution)/shard_map/wps,wpt->wst/dot_general | solution.py:27
  481.3 0.0 all-reduce.2.cloned.1.call-update
  481.4 64.4 %all-reduce.2.cloned.1.call-done = f32[8,256,256]{2,1,0:T(8,128)} async-done(((f32[8,256,256]{2,1,0:T(8,128)}), f32[8,256,256]{2,1,0:T(8,128)}) %all-reduce.2.cloned.1.call-update) | async-done | bytes 2097168 | tf_op jit(solution)/shard_map/psum | solution.py:51
  545.8 3.1 broadcast_multiply_fusion
  (7 shorter events, 0.1 us)
Async XLA Ops:
  8.7 19.5 %all-to-all-start.1 = ((bf16[16,1,128]{2,1,0:T(2,128)(2,1)}), bf16[16,1,128]{2,1,0:T(2,128)(2,1)S(1)}, u32[]{:S(2)}, u32[]{:S(2)}) async-start(bf16[16,1,128]{2,1,0:T(2,128)(2,1)} %copy.20), calls=%async_computation.1 | async-start | bytes 16384 | tf_op jit(solution)/shard_map/all_to_all | solution.py:46
  28.2 41.2 %all-to-all-start.2 = ((bf16[16,256,256]{2,1,0:T(8,128)(2,1)}), bf16[16,256,256]{2,1,0:T(8,128)(2,1)S(1)}, u32[]{:S(2)}, u32[]{:S(2)}) async-start(bf16[16,256,256]{2,1,0:T(8,128)(2,1)} %scatter_fusion.2), calls=%async_computation.2 | async-start | bytes 4194304 | tf_op jit(solution)/shard_map/all_to_all | solution.py:45
  69.5 377.3 %all-to-all-start = ((bf16[16,3072,256]{2,1,0:T(8,128)(2,1)}), bf16[16,3072,256]{2,1,0:T(8,128)(2,1)}, u32[]{:S(2)}, u32[]{:S(2)}) async-start(bf16[16,3072,256]{2,1,0:T(8,128)(2,1)} %scatter_fusion), calls=%async_computation | async-start | bytes 50331648 | tf_op jit(solution)/shard_map/all_to_all | solution.py:44
  76.9 468.9 %all-reduce.2.cloned.1.call-start = ((), (), s32[]{:S(2)}) async-start(), calls=%async_computation.3 | async-start | bytes 4194304 | tf_op jit(solution)/shard_map/psum | solution.py:51
Sparse Core Ops, SparseCore 0:
  481.5 64.2 all-reduce.1
where the time goes:
time: 556 us
  waiting for transfers between devices  434 us (78%)
  local copies, waits for them, and re-layouts  55.9 us (10%)
  starting transfers between devices  22.8 us (4%)
  matrix products  19.9 us (4%)
  between operations  13.5 us (2%)
  other arithmetic  9.96 us (2%)
    all_to_all x1, waiting for transfers between devices, on_device(): lax.all_to_all(vec_buf, 'win', split_axis=0, concat_axis=0, tiled=True)  369 us
    psum x1, waiting for transfers between devices, on_device(): total = lax.psum(partial_value, 'space')  64.4 us
    scatter x1, local copies, waits for them, and re-layouts, on_device(): jnp.zeros((nblocks,) + modes.shape[1:], jnp.bfloat16).at[dest].set(modes)  25.7 us
    dot_general x1, matrix products, batch_grams(): jnp.einsum('wps,wpt->wst', resid, resid, preferred_element_type=jnp.float32)  19.9 us
    gather x2, local copies, waits for them, and re-layouts, on_device(): partial_value = batch_grams(snapshots, got_vec[source], got_coef[source])  15.2 us
  transfers between devices with their start and end apart: 4, of which 2 were waited for; matrix products, arithmetic and copies ran while one was open for 8% of the time, Pallas kernels for 0%

commit v1 on v0

--- a/solution.py
+++ b/solution.py
@@ -48,7 +48,9 @@
     marks = got_mark[:, :WIN_DEV].astype(jnp.int32)
     source = jnp.sum(jnp.arange(nblocks, dtype=jnp.int32)[:, None] * marks, axis=0)
     partial_value = batch_grams(snapshots, got_vec[source], got_coef[source])
-    total = lax.psum(partial_value, "space")
+    total = partial_value
+    for hop in (1, 2, 4):
+        total = total + lax.ppermute(total, "space", [(dev, dev ^ hop) for dev in range(8)])
     return total / points_all
 
 

time: 556 us -> 582 us (1.047)
  waiting for transfers between devices: 434 us -> 465 us
  between operations: 13.5 us -> 0.13 us
    ppermute x0 -> x3, waiting for transfers between devices: none -> 95.6 us  [on_device(): lax.ppermute(total, 'space', [(dev, dev ^ hop) for dev in range(8)])]
    psum x1 -> x0, waiting for transfers between devices: 64.4 us -> none  [on_device(): total = lax.psum(partial_value, 'space')]
  transfers between devices with their start and end apart: 4 -> 6, of which waited for: 2 -> 4; matrix products, arithmetic and copies ran while one was open for 8% -> 8% of each run, Pallas kernels for 0% -> 0%
where the time goes in v1:
time: 582 us
  waiting for transfers between devices  465 us (80%)
  local copies, waits for them, and re-layouts  55.9 us (10%)
  starting transfers between devices  27.5 us (5%)
  matrix products  24.3 us (4%)
  other arithmetic  9.2 us (2%)
    all_to_all x1, waiting for transfers between devices, on_device(): lax.all_to_all(vec_buf, 'win', split_axis=0, concat_axis=0, tiled=True)  369 us
    ppermute x3, waiting for transfers between devices, on_device(): lax.ppermute(total, 'space', [(dev, dev ^ hop) for dev in range(8)])  95.6 us
    scatter x1, local copies, waits for them, and re-layouts, on_device(): jnp.zeros((nblocks,) + modes.shape[1:], jnp.bfloat16).at[dest].set(modes)  25.7 us
    dot_general x1, matrix products, batch_grams(): jnp.einsum('wps,wpt->wst', resid, resid, preferred_element_type=jnp.float32)  24.3 us
    gather x2, local copies, waits for them, and re-layouts, on_device(): partial_value = batch_grams(snapshots, got_vec[source], got_coef[source])  15.2 us
  transfers between devices with their start and end apart: 6, of which 4 were waited for; matrix products, arithmetic and copies ran while one was open for 8% of the time, Pallas kernels for 0%

profile of v1, /device:TPU:0, one launch (start us, length us, event | category | flops | bytes accessed | tf_op | source)
XLA Modules:
  0.0 582.0 jit_solution(14621070001733090956)
XLA Ops:
  0.0 0.7 fusion.18
  0.7 0.9 scatter_fusion.1
  1.6 0.6 copy.20
  2.2 8.2 %all-to-all-start.1 = ((bf16[16,1,128]{2,1,0:T(2,128)(2,1)}), bf16[16,1,128]{2,1,0:T(2,128)(2,1)S(1)}, u32[]{:S(2)}, u32[]{:S(2)}) async-start(bf16[16,1,128]{2,1,0:T(2,128)(2,1)} %copy.20), calls=%async_computation.1 | async-start | bytes 16384 | tf_op jit(solution)/shard_map/all_to_all | solution.py:46
  10.3 0.7 fusion.14
  11.1 5.3 fusion.9
  16.4 0.1 pad_maximum_fusion
  16.5 0.6 copy.21
  17.1 0.2 copy.22
  17.3 1.5 broadcast_in_dim.14
  18.9 2.8 scatter_fusion.2
  21.7 0.0 all-to-all-done.1
  21.7 7.2 %all-to-all-start.2 = ((bf16[16,256,256]{2,1,0:T(8,128)(2,1)}), bf16[16,256,256]{2,1,0:T(8,128)(2,1)S(1)}, u32[]{:S(2)}, u32[]{:S(2)}) async-start(bf16[16,256,256]{2,1,0:T(8,128)(2,1)} %scatter_fusion.2), calls=%async_computation.2 | async-start | bytes 4194304 | tf_op jit(solution)/shard_map/all_to_all | solution.py:45
  28.9 8.4 %broadcast_in_dim.10 = bf16[16,3072,256]{2,1,0:T(8,128)(2,1)} broadcast(bf16[]{:T(256)} %constant.32.clone.1), dimensions={} | broadcast | bytes 25165826 | tf_op jit(solution)/shard_map/broadcast_in_dim | solution.py:36
  37.3 25.7 %scatter_fusion = bf16[16,3072,256]{2,1,0:T(8,128)(2,1)} fusion(bf16[16,3072,256]{2,1,0:T(8,128)(2,1)} %broadcast_in_dim.10, s32[8]{0:T(128)S(1)} %get-tuple-element.6, bf16[8,3072,256]{2,1,0:T(8,128)(2,1)} %param.9), kind=kCustom, calls=%fused_computation.2 | custom fusion | bytes 37748768 | tf_op jit(solution)/shard_map/scatter | solution.py:36
  62.9 0.0 all-to-all-done.2
  62.9 7.4 %all-to-all-start = ((bf16[16,3072,256]{2,1,0:T(8,128)(2,1)}), bf16[16,3072,256]{2,1,0:T(8,128)(2,1)}, u32[]{:S(2)}, u32[]{:S(2)}) async-start(bf16[16,3072,256]{2,1,0:T(8,128)(2,1)} %scatter_fusion), calls=%async_computation | async-start | bytes 50331648 | tf_op jit(solution)/shard_map/all_to_all | solution.py:44
  70.4 0.6 gather_fusion.1
  71.0 369.3 %all-to-all-done = bf16[16,3072,256]{2,1,0:T(8,128)(2,1)} async-done(((bf16[16,3072,256]{2,1,0:T(8,128)(2,1)}), bf16[16,3072,256]{2,1,0:T(8,128)(2,1)}, u32[]{:S(2)}, u32[]{:S(2)}) %all-to-all-start) | async-done | bytes 25165856 | tf_op jit(solution)/shard_map/all_to_all | solution.py:44
  440.3 14.6 %gather_fusion = bf16[8,3072,256]{2,1,0:T(8,128)(2,1)} fusion(bf16[16,3072,256]{2,1,0:T(8,128)(2,1)} %all-to-all-done, s32[1024]{0:T(1024)S(1)} %pad_clamp_fusion), kind=kCustom, calls=%fused_computation | custom fusion | bytes 25165856 | tf_op jit(solution)/shard_map/gather | solution.py:50
  454.9 24.3 %fusion = f32[8,256,256]{2,1,0:T(8,128)S(1)} fusion(bf16[8,3072,256]{2,1,0:T(8,128)(2,1)} %param.8, bf16[8,3072,256]{2,1,0:T(8,128)(2,1)} %gather_fusion, bf16[8,256,256]{2,1,0:T(8,128)(2,1)S(1)} %gather_fusion.1), kind=kOutput, calls=%fused_computation.6 | convolution fusion | flops 6461325312 | bytes 28311552 | tf_op jit(solution)/shard_map/wps,wpt->wst/dot_general | solution.py:27
  479.2 0.1 collective-permute-start
  479.3 4.1 collective-permute-done
  483.5 0.4 add.50
  483.9 1.6 collective-permute-start.1
  485.4 46.2 %collective-permute-done.1 = f32[8,256,256]{2,1,0:T(8,128)S(1)} collective-permute-done((f32[8,256,256]{2,1,0:T(8,128)S(1)}, f32[8,256,256]{2,1,0:T(8,128)S(1)}, u32[]{:S(2)}, u32[]{:S(2)}) %collective-permute-start.1) | collective-permute-done | bytes 2097184 | tf_op jit(solution)/shard_map/ppermute | solution.py:53
  531.6 0.3 add.51
  531.9 3.1 collective-permute-start.2
  535.0 45.3 %collective-permute-done.2 = f32[8,256,256]{2,1,0:T(8,128)S(1)} collective-permute-done((f32[8,256,256]{2,1,0:T(8,128)S(1)}, f32[8,256,256]{2,1,0:T(8,128)S(1)}, u32[]{:S(2)}, u32[]{:S(2)}) %collective-permute-start.2) | collective-permute-done | bytes 2097184 | tf_op jit(solution)/shard_map/ppermute | solution.py:53
  580.3 1.7 add_multiply_fusion
  (7 shorter events, 0.1 us)
Async XLA Ops:
  2.2 19.5 %all-to-all-start.1 = ((bf16[16,1,128]{2,1,0:T(2,128)(2,1)}), bf16[16,1,128]{2,1,0:T(2,128)(2,1)S(1)}, u32[]{:S(2)}, u32[]{:S(2)}) async-start(bf16[16,1,128]{2,1,0:T(2,128)(2,1)} %copy.20), calls=%async_computation.1 | async-start | bytes 16384 | tf_op jit(solution)/shard_map/all_to_all | solution.py:46
  21.7 41.2 %all-to-all-start.2 = ((bf16[16,256,256]{2,1,0:T(8,128)(2,1)}), bf16[16,256,256]{2,1,0:T(8,128)(2,1)S(1)}, u32[]{:S(2)}, u32[]{:S(2)}) async-start(bf16[16,256,256]{2,1,0:T(8,128)(2,1)} %scatter_fusion.2), calls=%async_computation.2 | async-start | bytes 4194304 | tf_op jit(solution)/shard_map/all_to_all | solution.py:45
  62.9 377.3 %all-to-all-start = ((bf16[16,3072,256]{2,1,0:T(8,128)(2,1)}), bf16[16,3072,256]{2,1,0:T(8,128)(2,1)}, u32[]{:S(2)}, u32[]{:S(2)}) async-start(bf16[16,3072,256]{2,1,0:T(8,128)(2,1)} %scatter_fusion), calls=%async_computation | async-start | bytes 50331648 | tf_op jit(solution)/shard_map/all_to_all | solution.py:44
  479.2 4.2 collective-permute-start
  483.9 47.8 %collective-permute-start.1 = (f32[8,256,256]{2,1,0:T(8,128)S(1)}, f32[8,256,256]{2,1,0:T(8,128)S(1)}, u32[]{:S(2)}, u32[]{:S(2)}) collective-permute-start(f32[8,256,256]{2,1,0:T(8,128)S(1)} %add.50), channel_id=1, source_target_pairs={{0,32},{16,48},{32,0},{48,16},{64,96},{80,112},{96,64},{112,80},{1... | collective-permute-start | bytes 6291464 | tf_op jit(solution)/shard_map/ppermute | solution.py:53
  531.9 48.4 %collective-permute-start.2 = (f32[8,256,256]{2,1,0:T(8,128)S(1)}, f32[8,256,256]{2,1,0:T(8,128)S(1)}, u32[]{:S(2)}, u32[]{:S(2)}) collective-permute-start(f32[8,256,256]{2,1,0:T(8,128)S(1)} %add.51), channel_id=1, source_target_pairs={{0,64},{16,80},{32,96},{48,112},{64,0},{80,16},{96,32},{112,48},{1... | collective-permute-start | bytes 6291464 | tf_op jit(solution)/shard_map/ppermute | solution.py:53
